TPU v7x, 256 devices: a whole 4x4x8 slice. The times are simulated.
256 devices in a mesh: pb: 64 (over x, z, core), ka: 4 (over y).
Axes of the slice: x: 4, y: 4, z: 8, core: 2. Of those that a mesh axis runs over, the one named last changes fastest.
Arguments:
- valence: float32 [1664, 64, 1024], P('pb', 'ka'), may hold values from -6 to 6
- conduction: bfloat16 [1664, 196, 1024], P('pb', None, 'ka'), may hold values from -0.0024414062 to 0.0024414062
- screened: float32 [64, 1024, 1024], P('pb'), may hold values from -1 to 3, as said below
- momentum: int32 [1664, 1], P('pb'), may hold values from 0 to 63; in each aligned block of 26 rows (0 to 25, 26 to 51, ...) at most 2 rows name the same one
- kpairs: int32 [1664, 2], P('pb'), may hold values from 0 to 63
- kpoint_slot: int32 [64], replicated, may hold values from 0 to 63, each once
- trial_blocks: float32 [64, 14336], P('pb', 'ka'), may hold values from -6 to 6
Outputs:
- response: float32 [64, 14336], P('pb', 'ka')
Inputs may be any that keep to these rules, and one draw needn't show every extreme that they name: Among the k-pairs of one index of pb (rows i * 26 to (i + 1) * 26 - 1), at most 2 share a momentum transfer. `kpoint_slot`: each row number appears once. `screened`: each matrix is symmetric.
All inputs are finite; a program needn't handle non-finite values.
Results may differ from a plain program's by a relative error of at most 0.0003.
Values sent between devices are 32-bit elements; how exact they have to be, the bound alone decides.
No kernel may reach another device: no remote copies, remote signals or barrier semaphores. Data moves between devices by JAX's collectives and lax.ppermute only.
A program may use at most 128 MiB of HBM per device.

v0:
```python
import jax
import jax.numpy as jnp
from jax import lax
from jax.sharding import PartitionSpec as P

VB = 8
CB = 14


def local(valence, conduction, screened, momentum, kpairs, kpoint_slot, trial_blocks):
    highest = lax.Precision.HIGHEST
    pair_dev = valence.shape[0]
    owners = lax.axis_size("pb")
    capacity = max(2, 2 * pair_dev // owners)
    slot_count = owners * capacity
    target = momentum[:, 0]
    indices = jnp.arange(pair_dev, dtype=jnp.int32)
    earlier = (target[:, None] == target[None, :]) & (indices[None, :] < indices[:, None])
    position = target * capacity + jnp.sum(earlier.astype(jnp.int32), axis=1)
    matches = position[None, :] == jnp.arange(slot_count, dtype=jnp.int32)[:, None]
    source = jnp.sum(jnp.where(matches, indices[None, :], 0), axis=1)
    filled = jnp.any(matches, axis=1)
    outgoing = jnp.where(filled[:, None, None], jnp.take(valence, source, axis=0), 0.0)
    outgoing = outgoing.reshape(owners, capacity, valence.shape[1], valence.shape[2])
    matrix = screened[0]
    product = jnp.einsum(
        "scrg,gh->scrh",
        lax.all_to_all(outgoing, "pb", split_axis=0, concat_axis=0, tiled=True),
        matrix,
        precision=highest,
        preferred_element_type=jnp.float32,
    )
    returned = lax.all_to_all(
        lax.all_to_all(product, "pb", split_axis=0, concat_axis=0, tiled=True),
        "ka",
        split_axis=3,
        concat_axis=2,
        tiled=True,
    )
    by_slot = returned.reshape(slot_count, returned.shape[2], returned.shape[3])
    columns = jnp.take(by_slot, position, axis=0)
    conduct_wide = conduction.astype(jnp.float32)
    partial_kernel = jnp.einsum(
        "prg,pbg->prb", columns, conduct_wide, precision=highest, preferred_element_type=jnp.float32
    )
    kernel = lax.psum(partial_kernel, "ka")
    gathered = lax.all_gather(trial_blocks, "pb", axis=0, tiled=True)
    kpoint_count = gathered.shape[0]
    local_trials = gathered.shape[1] // (VB * CB)
    blocks = gathered.reshape(kpoint_count, local_trials, VB, CB)
    slot_near = jnp.take(kpoint_slot, kpairs[:, 0])
    slot_far = jnp.take(kpoint_slot, kpairs[:, 1])
    near_trials = jnp.take(blocks, slot_near, axis=0)
    far_trials = jnp.take(blocks, slot_far, axis=0)
    kernel_blocks = kernel.reshape(pair_dev, VB, VB, CB, CB)
    direct = jnp.einsum("pvwcd,pnwd->pnvc", kernel_blocks, far_trials, precision=highest)
    mirror = jnp.einsum("pvwcd,pnvc->pnwd", kernel_blocks, near_trials, precision=highest)
    kpoint_rows = jnp.arange(kpoint_count, dtype=jnp.int32)[:, None]
    onehot_near = (slot_near[None, :] == kpoint_rows).astype(jnp.float32)
    onehot_far = (slot_far[None, :] == kpoint_rows).astype(jnp.float32)
    summed = jnp.dot(
        onehot_near,
        direct.reshape(pair_dev, -1),
        precision=highest,
        preferred_element_type=jnp.float32,
    )
    summed = summed + jnp.dot(
        onehot_far,
        mirror.reshape(pair_dev, -1),
        precision=highest,
        preferred_element_type=jnp.float32,
    )
    return lax.psum_scatter(summed, "pb", scatter_dimension=0, tiled=True)


def solution(mesh):
    return jax.shard_map(
        local,
        mesh=mesh,
        in_specs=(
            P("pb", "ka", None),
            P("pb", None, "ka"),
            P("pb", None, None),
            P("pb", None),
            P("pb", None),
            P(),
            P("pb", "ka"),
        ),
        out_specs=P("pb", "ka"),
        check_vma=False,
    )
```

profile of v0, /device:TPU:8, one launch (start us, length us, event | category | flops | bytes accessed | tf_op | source)
XLA Modules:
  0.0 1163.5 jit_solution(17893508544063465319)
XLA Ops:
  8.7 5.8 gather_fusion
  18.5 198.0 %all_to_all.25 = f32[64,2,16,1024]{3,2,1,0:T(8,128)S(1)} all-to-all(f32[64,2,16,1024]{3,2,1,0:T(8,128)S(1)} %select_select_fusion), channel_id=1, replica_groups=mesh['pb'=64,'ka'=4] {'pb'}, dimensions={0} | all-to-all | bytes 16777216 | tf_op jit(solution)/shard_map/all_to_all | solution.py:28
  216.4 27.7 %fusion = f32[64,2,16,1024]{3,2,1,0:T(8,128)S(1)} fusion(f32[64,2,16,1024]{3,2,1,0:T(8,128)S(1)} %all_to_all.25, f32[1,1024,1024]{2,1,0:T(8,128)S(1)} %copy-done.5), kind=kOutput, calls=%fused_computation.8 | convolution fusion | flops 25769803776 | bytes 20971520 | tf_op jit(solution)/shard_map/scrg,gh->scrh/dot_general | solution.py:26
  244.1 192.1 %all_to_all.26 = f32[64,2,16,1024]{3,2,1,0:T(8,128)} all-to-all(f32[64,2,16,1024]{3,2,1,0:T(8,128)S(1)} %fusion), channel_id=1, replica_groups=mesh['pb'=64,'ka'=4] {'pb'}, dimensions={0} | all-to-all | bytes 16777216 | tf_op jit(solution)/shard_map/all_to_all | solution.py:34
  436.2 16.3 %copy.61 = f32[64,2,16,1024]{0,2,1,3:T(8,128)} copy(f32[64,2,16,1024]{3,2,1,0:T(8,128)} %all_to_all.26) | data formatting | bytes 16777216 | tf_op jit(solution)/shard_map/all_to_all | solution.py:34
  452.5 14.3 %reshape.142 = f32[4,1,524288]{2,1,0:T(1,128)} reshape(f32[1024,2,16,64]{3,2,1,0:T(8,128)} %bitcast.68) | data formatting | bytes 16777216
  466.8 6.2 all-to-all-start.2
  473.0 92.9 %all-to-all-done.2 = f32[4,1,524288]{2,1,0:T(1,128)} async-done(((f32[4,1,524288]{2,1,0:T(1,128)}), f32[4,1,524288]{2,1,0:T(1,128)}, u32[]{:S(2)}, u32[]{:S(2)}) %all-to-all-start.2) | async-done | bytes 8388640 | tf_op jit(solution)/shard_map/all_to_all | solution.py:33
  566.5 30.1 %reduce = f32[4,524288]{1,0:T(4,128)} reduce(f32[4,1,524288]{2,1,0:T(1,128)} %all-to-all-done.2, f32[]{:T(128)} %broadcast.181), dimensions={1}, to_apply=%all_to_all.19.reduce_sub_computation | reduce | bytes 16777220 | tf_op jit(solution)/shard_map/all_to_all | solution.py:33
  596.6 16.8 %reshape.143 = f32[1024,2,16,64]{3,2,1,0:T(8,128)} reshape(f32[4,524288]{1,0:T(4,128)} %reduce) | data formatting | bytes 16777216
  613.4 14.4 %copy.75 = f32[64,2,16,4,256]{4,3,2,1,0:T(4,128)} copy(f32[64,2,16,4,256]{0,2,1,4,3:T(8,128)} %bitcast.69) | data formatting | bytes 16777216 | tf_op jit(solution)/shard_map/all_to_all | solution.py:33
  627.8 8.6 copy.63
  636.4 5.3 gather_fusion.1
  641.7 5.3 fusion.2
  647.0 5.8 copy.64
  652.8 14.5 %copy.65 = f32[26,8,8,14,14]{3,2,4,1,0:T(8,128)} copy(f32[26,8,8,14,14]{0,2,1,4,3:T(8,128)} %bitcast.72) | data formatting | bytes 2609152 | tf_op jit(solution)/shard_map/reshape | solution.py:55
  669.4 52.6 %all-gather = f32[64,1,3584]{2,1,0:T(1,128)} all-gather(f32[1,1,3584]{2,1,0:T(1,128)S(1)} %bitcast.74), channel_id=1, replica_groups=mesh['pb'=64,'ka'=4] {'pb'}, dimensions={0}, use_global_device_ids=true | all-gather | bytes 931840 | tf_op jit(solution)/shard_map/all_gather | solution.py:47
  728.7 5.5 copy.60
  741.9 142.4 %all-reduce.4.cloned.1.call-done = f32[26,8,8,14,14]{3,2,4,1,0:T(8,128)} async-done(((f32[26,8,8,14,14]{3,2,4,1,0:T(8,128)}), f32[26,8,8,14,14]{3,2,4,1,0:T(8,128)}) %all-reduce.4.cloned.1.call-update) | async-done | bytes 1304592 | tf_op jit(solution)/shard_map/psum | solution.py:46
  884.3 16.3 %copy.68 = f32[26,8,8,14,14]{4,1,3,2,0:T(8,128)} copy(f32[26,8,8,14,14]{3,2,4,1,0:T(8,128)} %all-reduce.4.cloned.1.call-done) | data formatting | bytes 2609152 | tf_op jit(solution)/shard_map/psum | solution.py:46
  900.7 22.8 %convolution_bitcast_fusion = f32[26,32,8,14]{1,3,2,0:T(8,128)} fusion(f32[26,8,8,14,14]{4,1,3,2,0:T(8,128)} %copy.68, f32[26,32,8,14]{1,2,3,0:T(8,128)} %gather_fusion.5, pred[26]{0:T(512)(128)(4,1)S(1)} %get-tuple-element.6), kind=kOutput, calls=%fused_computation.12 | convolution fusion | flops 125332480 | bytes 2050074 | tf_op jit(solution)/shard_map/pvwcd,pnvc->pnwd/dot_general | solution.py:57
  931.2 23.0 %convolution_bitcast_fusion.1 = f32[26,32,8,14]{1,3,2,0:T(8,128)} fusion(f32[26,8,8,14,14]{3,2,4,1,0:T(8,128)} %all-reduce.4.cloned.1.call-done, f32[26,32,8,14]{1,2,3,0:T(8,128)} %gather_fusion.4, pred[26]{0:T(512)(128)(4,1)S(1)} %get-tuple-element.13), kind=kOutput, calls=%fused_computation.13 | convolution fusion | flops 125332480 | bytes 2050074 | tf_op jit(solution)/shard_map/pvwcd,pnwd->pnvc/dot_general | solution.py:56
  957.9 4.6 reshape.71
  966.2 188.0 %all-reduce.6.cloned.1.call-done = f32[64,3584]{1,0:T(8,128)} async-done(((f32[64,3584]{1,0:T(8,128)}), f32[64,3584]{1,0:T(8,128)}) %all-reduce.6.cloned.1.call-update) | async-done | bytes 917520
  (51 shorter events, 40.4 us)
Async XLA Ops:
  6.5 635.1 %copy-start = (bf16[26,196,256]{2,1,0:T(8,128)(2,1)S(1)}, bf16[26,196,256]{2,1,0:T(8,128)(2,1)}, u32[]{:S(2)}) copy-start(bf16[26,196,256]{2,1,0:T(8,128)(2,1)} %param.12) | copy-start | bytes 7827460
  18.4 198.0 %copy-start.5 = (f32[1,1024,1024]{2,1,0:T(8,128)S(1)}, f32[1,1024,1024]{2,1,0:T(8,128)}, u32[]{:S(2)}) copy-start(f32[1,1024,1024]{2,1,0:T(8,128)} %param.13) | copy-start | bytes 12582916
  466.8 6.2 copy-start.4
  466.8 99.1 %all-to-all-start.2 = ((f32[4,1,524288]{2,1,0:T(1,128)}), f32[4,1,524288]{2,1,0:T(1,128)}, u32[]{:S(2)}, u32[]{:S(2)}) async-start(f32[4,1,524288]{2,1,0:T(1,128)} %reshape.142), calls=%async_computation.2 | async-start | bytes 16777216 | tf_op jit(solution)/shard_map/all_to_all | solution.py:33
  473.0 411.3 %all-reduce.4.cloned.1.call-start = ((), (), s32[]{:S(2)}) async-start(), calls=%async_computation.3 | async-start | bytes 23855104 | tf_op jit(solution)/shard_map/psum | solution.py:46
  667.3 0.7 copy-start.3
  667.3 0.7 copy-start.1
  667.3 2.1 copy-start.2
  667.3 486.9 %all-reduce.6.cloned.1.call-start = ((), (), s32[]{:S(2)}) async-start(), calls=%async_computation.4 | async-start | bytes 1835008
  957.9 7.6 copy-start.6
Sparse Core Ops, SparseCore 0:
  667.4 216.8 all-reduce.3
  965.7 188.5 all-reduce.5
where the time goes:
time: 1170 us; the launch traced here: 1160 us
  blocking collectives  443 us (38%)
  waiting for transfers between devices  423 us (36%)
  local copies, waits for them, and re-layouts  160 us (14%)
  matrix products  81.8 us (7%)
  other arithmetic  36 us (3%)
  between operations  13.8 us (1%)
    all_to_all x1, blocking collectives, local(): lax.all_to_all(outgoing, 'pb', split_axis=0, concat_axis=0, tiled=True)  198 us
    all_to_all x1, blocking collectives, local(): lax.all_to_all(product, 'pb', split_axis=0, concat_axis=0, tiled=True)  192 us
    unnamed x3, waiting for transfers between devices  188 us
    psum x1, waiting for transfers between devices, local(): kernel = lax.psum(partial_kernel, 'ka')  142 us
    all_to_all x1, waiting for transfers between devices, local(): lax.all_to_all(lax.all_to_all(product, 'pb', split_axis=0, concat_axis=0,...  92.9 us
    all_gather x1, blocking collectives, local(): gathered = lax.all_gather(trial_blocks, 'pb', axis=0, tiled=True)  52.6 us
    unnamed x18, local copies, waits for them, and re-layouts  34.6 us
    all_to_all x1, other arithmetic, local(): lax.all_to_all(lax.all_to_all(product, 'pb', split_axis=0, concat_axis=0,...  30.1 us
  transfers between devices with their start and end apart: 3, of which 3 were waited for; matrix products, arithmetic and copies ran while one was open for 2% of the time, Pallas kernels for 0%

commit v1 on v0

--- a/solution.py
+++ b/solution.py
@@ -5,6 +5,14 @@
 
 VB = 8
 CB = 14
+
+
+def doubling_sum(block, mesh_axis):
+    size, total = (lax.axis_size(mesh_axis), block)
+    for far in [1 << k for k in range(size.bit_length() - 1)]:
+        pairs = [(i, i ^ far) for i in range(size)]
+        total = total + lax.ppermute(total, mesh_axis, pairs)
+    return total
 
 
 def local(valence, conduction, screened, momentum, kpairs, kpoint_slot, trial_blocks):
@@ -43,7 +51,7 @@
     partial_kernel = jnp.einsum(
         "prg,pbg->prb", columns, conduct_wide, precision=highest, preferred_element_type=jnp.float32
     )
-    kernel = lax.psum(partial_kernel, "ka")
+    kernel = doubling_sum(partial_kernel, "ka")
     gathered = lax.all_gather(trial_blocks, "pb", axis=0, tiled=True)
     kpoint_count = gathered.shape[0]
     local_trials = gathered.shape[1] // (VB * CB)

time: 1170 us -> 1070 us (0.915)
  waiting for transfers between devices: 423 us -> 313 us
    psum x1 -> x0, waiting for transfers between devices: 142 us -> none  [local(): kernel = lax.psum(partial_kernel, 'ka')]
    ppermute x0 -> x2, waiting for transfers between devices: none -> 37 us  [doubling_sum(): total = total + lax.ppermute(total, mesh_axis, pairs)]
    psum x1 -> x0, local copies, waits for them, and re-layouts: 16.3 us -> none  [local(): kernel = lax.psum(partial_kernel, 'ka')]
    reshape x1 -> x2, local copies, waits for them, and re-layouts: 14.5 us -> 29.1 us  [local(): kernel_blocks = kernel.reshape(pair_dev, VB, VB, CB, CB)]
    unnamed x3 -> x2, waiting for transfers between devices: 188 us -> 183 us
  transfers between devices with their start and end apart: 3 -> 4, of which waited for: 3 -> 3; matrix products, arithmetic and copies ran while one was open for 2% -> 2% of each run, Pallas kernels for 0% -> 0%
where the time goes in v1:
time: 1070 us; the launch traced here: 1060 us
  blocking collectives  444 us (41%)
  waiting for transfers between devices  313 us (29%)
  local copies, waits for them, and re-layouts  157 us (15%)
  matrix products  81.5 us (8%)
  other arithmetic  41.1 us (4%)
  between operations  13.8 us (1%)
    all_to_all x1, blocking collectives, local(): lax.all_to_all(outgoing, 'pb', split_axis=0, concat_axis=0, tiled=True)  198 us
    all_to_all x1, blocking collectives, local(): lax.all_to_all(product, 'pb', split_axis=0, concat_axis=0, tiled=True)  192 us
    unnamed x2, waiting for transfers between devices  183 us
    all_to_all x1, waiting for transfers between devices, local(): lax.all_to_all(lax.all_to_all(product, 'pb', split_axis=0, concat_axis=0,...  92.9 us
    all_gather x1, blocking collectives, local(): gathered = lax.all_gather(trial_blocks, 'pb', axis=0, tiled=True)  54.2 us
    ppermute x2, waiting for transfers between devices, doubling_sum(): total = total + lax.ppermute(total, mesh_axis, pairs)  37 us
    unnamed x18, local copies, waits for them, and re-layouts  34 us
    all_to_all x1, other arithmetic, local(): lax.all_to_all(lax.all_to_all(product, 'pb', split_axis=0, concat_axis=0,...  30.1 us
  transfers between devices with their start and end apart: 4, of which 3 were waited for; matrix products, arithmetic and copies ran while one was open for 2% of the time, Pallas kernels for 0%

profile of v1, /device:TPU:8, one launch (start us, length us, event | category | flops | bytes accessed | tf_op | source)
XLA Modules:
  0.0 1059.6 jit_solution(545944887493288051)
XLA Ops:
  8.7 5.8 gather_fusion
  18.5 198.0 %all_to_all.25 = f32[64,2,16,1024]{3,2,1,0:T(8,128)S(1)} all-to-all(f32[64,2,16,1024]{3,2,1,0:T(8,128)S(1)} %select_select_fusion), channel_id=1, replica_groups=mesh['pb'=64,'ka'=4] {'pb'}, dimensions={0} | all-to-all | bytes 16777216 | tf_op jit(solution)/shard_map/all_to_all | solution.py:36
  216.4 27.7 %fusion = f32[64,2,16,1024]{3,2,1,0:T(8,128)S(1)} fusion(f32[64,2,16,1024]{3,2,1,0:T(8,128)S(1)} %all_to_all.25, f32[1,1024,1024]{2,1,0:T(8,128)S(1)} %copy-done.5), kind=kOutput, calls=%fused_computation.8 | convolution fusion | flops 25769803776 | bytes 20971520 | tf_op jit(solution)/shard_map/scrg,gh->scrh/dot_general | solution.py:34
  244.1 192.1 %all_to_all.26 = f32[64,2,16,1024]{3,2,1,0:T(8,128)} all-to-all(f32[64,2,16,1024]{3,2,1,0:T(8,128)S(1)} %fusion), channel_id=1, replica_groups=mesh['pb'=64,'ka'=4] {'pb'}, dimensions={0} | all-to-all | bytes 16777216 | tf_op jit(solution)/shard_map/all_to_all | solution.py:42
  436.2 16.3 %copy.61 = f32[64,2,16,1024]{0,2,1,3:T(8,128)} copy(f32[64,2,16,1024]{3,2,1,0:T(8,128)} %all_to_all.26) | data formatting | bytes 16777216 | tf_op jit(solution)/shard_map/all_to_all | solution.py:42
  452.5 14.3 %reshape.142 = f32[4,1,524288]{2,1,0:T(1,128)} reshape(f32[1024,2,16,64]{3,2,1,0:T(8,128)} %bitcast.68) | data formatting | bytes 16777216
  466.8 6.2 all-to-all-start.2
  473.0 92.9 %all-to-all-done.2 = f32[4,1,524288]{2,1,0:T(1,128)} async-done(((f32[4,1,524288]{2,1,0:T(1,128)}), f32[4,1,524288]{2,1,0:T(1,128)}, u32[]{:S(2)}, u32[]{:S(2)}) %all-to-all-start.2) | async-done | bytes 8388640 | tf_op jit(solution)/shard_map/all_to_all | solution.py:41
  566.5 30.1 %reduce = f32[4,524288]{1,0:T(4,128)} reduce(f32[4,1,524288]{2,1,0:T(1,128)} %all-to-all-done.2, f32[]{:T(128)} %broadcast.181), dimensions={1}, to_apply=%all_to_all.19.reduce_sub_computation | reduce | bytes 16777220 | tf_op jit(solution)/shard_map/all_to_all | solution.py:41
  596.6 16.8 %reshape.143 = f32[1024,2,16,64]{3,2,1,0:T(8,128)} reshape(f32[4,524288]{1,0:T(4,128)} %reduce) | data formatting | bytes 16777216
  613.4 14.4 %copy.75 = f32[64,2,16,4,256]{4,3,2,1,0:T(4,128)} copy(f32[64,2,16,4,256]{0,2,1,4,3:T(8,128)} %bitcast.69) | data formatting | bytes 16777216 | tf_op jit(solution)/shard_map/all_to_all | solution.py:41
  627.8 8.6 copy.63
  636.4 5.3 gather_fusion.1
  641.7 4.1 fusion.2
  647.3 37.0 %collective-permute-done = f32[26,64,196]{2,1,0:T(8,128)S(1)} collective-permute-done((f32[26,64,196]{2,1,0:T(8,128)S(1)}, f32[26,64,196]{2,1,0:T(8,128)S(1)}, u32[]{:S(2)}, u32[]{:S(2)}) %collective-permute-start) | collective-permute-done | bytes 1304608 | tf_op jit(solution)/shard_map/ppermute | solution.py:14
  688.6 54.2 %all-gather = f32[64,1,3584]{2,1,0:T(1,128)} all-gather(f32[1,1,3584]{2,1,0:T(1,128)S(1)} %bitcast.75), channel_id=1, replica_groups=mesh['pb'=64,'ka'=4] {'pb'}, dimensions={0}, use_global_device_ids=true | all-gather | bytes 931840 | tf_op jit(solution)/shard_map/all_gather | solution.py:55
  742.8 4.0 copy.59
  749.5 5.5 copy.60
  766.1 5.7 copy.64
  771.9 14.5 %copy.65 = f32[26,8,8,14,14]{3,2,4,1,0:T(8,128)} copy(f32[26,8,8,14,14]{0,2,1,4,3:T(8,128)} %bitcast.70) | data formatting | bytes 2609152 | tf_op jit(solution)/shard_map/reshape | solution.py:63
  786.4 14.6 %copy.68 = f32[26,8,8,14,14]{4,1,3,2,0:T(8,128)} copy(f32[26,8,8,14,14]{0,2,1,4,3:T(8,128)} %bitcast.71) | data formatting | bytes 2609152 | tf_op jit(solution)/shard_map/reshape | solution.py:63
  801.0 22.8 %convolution_bitcast_fusion.1 = f32[26,32,8,14]{1,3,2,0:T(8,128)} fusion(f32[26,8,8,14,14]{3,2,4,1,0:T(8,128)} %copy.65, f32[26,32,8,14]{1,2,3,0:T(8,128)} %gather_fusion.4, pred[26]{0:T(512)(128)(4,1)S(1)} %get-tuple-element.13), kind=kOutput, calls=%fused_computation.13 | convolution fusion | flops 125332480 | bytes 2050074 | tf_op jit(solution)/shard_map/pvwcd,pnwd->pnvc/dot_general | solution.py:64
  833.1 22.8 %convolution_bitcast_fusion = f32[26,32,8,14]{1,3,2,0:T(8,128)} fusion(f32[26,8,8,14,14]{4,1,3,2,0:T(8,128)} %copy.68, f32[26,32,8,14]{1,2,3,0:T(8,128)} %gather_fusion.5, pred[26]{0:T(512)(128)(4,1)S(1)} %get-tuple-element.6), kind=kOutput, calls=%fused_computation.12 | convolution fusion | flops 125332480 | bytes 2050074 | tf_op jit(solution)/shard_map/pvwcd,pnvc->pnwd/dot_general | solution.py:65
  866.9 183.4 %all-reduce.3.cloned.1.call-done = f32[64,3584]{1,0:T(8,128)} async-done(((f32[64,3584]{1,0:T(8,128)}), f32[64,3584]{1,0:T(8,128)}) %all-reduce.3.cloned.1.call-update) | async-done | bytes 917520
  (54 shorter events, 48.6 us)
Async XLA Ops:
  6.5 635.1 %copy-start = (bf16[26,196,256]{2,1,0:T(8,128)(2,1)S(1)}, bf16[26,196,256]{2,1,0:T(8,128)(2,1)}, u32[]{:S(2)}) copy-start(bf16[26,196,256]{2,1,0:T(8,128)(2,1)} %param.12) | copy-start | bytes 7827460
  18.5 198.0 %copy-start.5 = (f32[1,1024,1024]{2,1,0:T(8,128)S(1)}, f32[1,1024,1024]{2,1,0:T(8,128)}, u32[]{:S(2)}) copy-start(f32[1,1024,1024]{2,1,0:T(8,128)} %param.13) | copy-start | bytes 12582916
  466.8 6.2 copy-start.4
  466.8 99.1 %all-to-all-start.2 = ((f32[4,1,524288]{2,1,0:T(1,128)}), f32[4,1,524288]{2,1,0:T(1,128)}, u32[]{:S(2)}, u32[]{:S(2)}) async-start(f32[4,1,524288]{2,1,0:T(1,128)} %reshape.142), calls=%async_computation.2 | async-start | bytes 16777216 | tf_op jit(solution)/shard_map/all_to_all | solution.py:41
  473.0 577.3 %all-reduce.3.cloned.1.call-start = ((), (), s32[]{:S(2)}) async-start(), calls=%async_computation.3 | async-start | bytes 1835008
  645.8 41.3 %copy-start.3 = (s32[26,2]{0,1:T(2,128)S(1)}, s32[26,2]{0,1:T(2,128)}, u32[]{:S(2)}) copy-start(s32[26,2]{0,1:T(2,128)} %param.15) | copy-start | bytes 628
  645.8 41.3 %copy-start.1 = (s32[64]{0:T(128)S(1)}, s32[64]{0:T(128)}, u32[]{:S(2)}) copy-start(s32[64]{0:T(128)} %param.16) | copy-start | bytes 772
  645.9 42.7 %copy-start.2 = (f32[1,3584]{1,0:T(1,128)S(1)}, f32[1,3584]{1,0:T(1,128)}, u32[]{:S(2)}) copy-start(f32[1,3584]{1,0:T(1,128)} %param.17) | copy-start | bytes 43012
  645.9 38.5 %collective-permute-start = (f32[26,64,196]{2,1,0:T(8,128)S(1)}, f32[26,64,196]{2,1,0:T(8,128)S(1)}, u32[]{:S(2)}, u32[]{:S(2)}) collective-permute-start(f32[26,64,196]{2,1,0:T(8,128)S(1)} %fusion.2), channel_id=1, source_target_pairs={{0,1},{1,0},{2,3},{3,2},{4,5},{5,4},{6,7},{7,6},{8,9},{9,8},{10,11... | collective-permute-start | bytes 3913736 | tf_op jit(solution)/shard_map/ppermute | solution.py:14
  685.8 76.8 %collective-permute-start.1 = (f32[26,64,196]{2,1,0:T(8,128)}, f32[26,64,196]{2,1,0:T(8,128)}, u32[]{:S(2)}, u32[]{:S(2)}) collective-permute-start(f32[26,64,196]{2,1,0:T(8,128)} %add.63), channel_id=1, source_target_pairs={{0,2},{1,3},{2,0},{3,1},{4,6},{5,7},{6,4},{7,5},{8,10},{9,11},{10,... | collective-permute-start | bytes 3913736 | tf_op jit(solution)/shard_map/ppermute | solution.py:14
  859.6 6.7 copy-start.6
Sparse Core Ops, SparseCore 0:
  866.4 183.9 all-reduce.2
